TPU v7x, 256 devices: a whole 4x4x8 slice. The times are simulated.
256 devices in a mesh: sky: 8 (over z), tm: 32 (over x, y, core).
Axes of the slice: x: 4, y: 4, z: 8, core: 2. Of those that a mesh axis runs over, the one named last changes fastest.
Arguments:
- tiles: float32 [4096, 128, 256], P(('sky', 'tm')), may hold values from -0.375 to 0.375
- tile_seg: int32 [4096], P(('sky', 'tm')), may hold values from 0 to 511, as said below
- tile_count: int32 [4096], P(('sky', 'tm')), may hold values from 32 to 128
- src_index: int32 [4096, 128], P(('sky', 'tm')), may hold values from 0 to 131071, as said below
- src_coef: float32 [5, 4096, 128], P(None, ('sky', 'tm')), may hold values from -6 to 6
- obs_weight: float32 [4096, 128], P(('sky', 'tm')), may hold values from 0.2 to 5
- att_dir: float32 [512, 256], P('tm'), may hold values from -6 to 6
- src_dir: float32 [5, 1048576], P(None, ('sky', 'tm')), may hold values from -6 to 6
Outputs:
- projected: float32 [4096, 128], P(('sky', 'tm'))
- att_normal: float32 [512, 256], P('tm')
- src_normal: float32 [5, 1048576], P(None, ('sky', 'tm'))
- curvature: float32 [], replicated
Inputs may be any that keep to these rules, and one draw needn't show every extreme that they name: `tile_seg`: within each aligned block of 16 tiles, at most 2 tiles name segments s with s // 16 equal to any one value; every block reaches 2 for some value. `src_index`: within each aligned block of 16 tiles, at most 128 observations name sources i with i // 4096 equal to any one value; every block reaches 128 for some value.
All inputs are finite; a program needn't handle non-finite values.
Results may differ from a plain program's by a relative error of at most 0.00011.
Values sent between devices are 32-bit elements; how exact they have to be, the bound alone decides.
A program may use at most 192 MiB of HBM per device.

v0:
```python
import jax
import jax.numpy as jnp
from jax import lax
from jax.sharding import PartitionSpec as P


def per_device(tiles, tile_seg, tile_count, src_index, src_coef, obs_weight, att_dir, src_dir):
    row_count = tiles.shape[1]
    params = src_coef.shape[0]
    row_ids = jnp.arange(row_count, dtype=jnp.int32)
    live_rows = row_ids[None, :] < tile_count[:, None]
    att_whole = lax.all_gather(att_dir, "tm", axis=0, tiled=True)
    src_region = lax.all_gather(src_dir, "tm", axis=1, tiled=True)
    seg_total = att_whole.shape[0]
    region_size = src_region.shape[1]
    seg_rows = att_whole[tile_seg]
    att_part = jnp.einsum("tjc,tc->tj", tiles, seg_rows, precision=lax.Precision.HIGHEST)
    picked = src_region[:, src_index]
    projected = jnp.where(
        live_rows, att_part + jnp.sum(src_coef * picked, axis=0), jnp.zeros_like(att_part)
    )
    weighted = obs_weight * projected
    curvature = lax.psum(jnp.sum(projected * weighted), ("sky", "tm"))
    tile_grad = jnp.einsum("tjc,tj->tc", tiles, weighted, precision=lax.Precision.HIGHEST)
    terms = (src_coef * weighted[None]).reshape(params, -1)
    src_terms = jax.ops.segment_sum(terms.T, src_index.reshape(-1), num_segments=region_size).T
    src_normal = lax.psum_scatter(src_terms, "tm", scatter_dimension=1, tiled=True)
    onehot = (tile_seg[:, None] == jnp.arange(seg_total, dtype=jnp.int32)[None, :]).astype(
        jnp.float32
    )
    seg_part = jnp.dot(
        onehot.T, tile_grad, precision=lax.Precision.HIGHEST, preferred_element_type=jnp.float32
    )
    owned = lax.psum_scatter(seg_part, "tm", scatter_dimension=0, tiled=True)
    att_normal = lax.psum(owned, "sky")
    return (projected, att_normal, src_normal, curvature)


def solution(mesh):
    placed = (
        P(("sky", "tm"), None, None),
        P(("sky", "tm")),
        P(("sky", "tm")),
        P(("sky", "tm"), None),
        P(None, ("sky", "tm"), None),
        P(("sky", "tm"), None),
        P("tm", None),
        P(None, ("sky", "tm")),
    )
    return jax.shard_map(
        per_device,
        mesh=mesh,
        in_specs=placed,
        out_specs=(P(("sky", "tm"), None), P("tm", None), P(None, ("sky", "tm")), P()),
        check_vma=False,
    )
```

profile of v0, /device:TPU:1, one launch (start us, length us, event | category | flops | bytes accessed | tf_op | source)
XLA Modules:
  0.0 777.7 jit_solution(14930510134184382425)
XLA Ops:
  7.2 0.0 copy-start
  7.2 0.0 copy-start.6
  7.2 0.0 copy-start.3
  7.2 0.0 copy-start.2
  7.2 0.0 all-gather.2.cloned.1.call-start
  7.3 3.0 copy.12
  10.3 0.0 all-gather.2.cloned.1.call-update
  10.3 0.0 reduce-scatter.3.cloned.1.call-start
  10.3 0.0 copy-done.6
  10.4 0.0 copy-done.3
  10.4 0.0 copy-start.1
  10.4 0.0 copy-start.4
  10.4 0.0 copy-start.5
  10.4 26.6 %all_gather.6 = f32[512,256]{1,0:T(8,128)S(1)} all-gather(f32[16,256]{1,0:T(8,128)S(1)} %copy-done.3), channel_id=1, replica_groups=mesh['sky'=8,'tm'=32] {'tm'}, dimensions={0}, use_global_device_ids=true | all-gather | bytes 540672 | tf_op jit(solution)/shard_map/all_gather | solution.py:12
  37.0 0.6 gather_fusion
  37.6 0.0 copy-done.2
  37.6 0.0 copy-done
  37.6 1.8 fusion.4
  39.5 181.6 %all-gather.2.cloned.1.call-done = f32[5,131072]{0,1:T(8,128)} async-done(((f32[5,4096]{0,1:T(8,128)}), f32[5,131072]{0,1:T(8,128)}) %all-gather.2.cloned.1.call-update) | async-done | bytes 2621456 | tf_op jit(solution)/shard_map/all_gather | solution.py:13
  221.1 20.4 %gather_fusion.1 = f32[2048,5]{1,0:T(8,128)S(1)} fusion(f32[5,131072]{0,1:T(8,128)} %all-gather.2.cloned.1.call-done, s32[2048]{0:T(1024)S(1)} %fusion.8), kind=kCustom, calls=%fused_computation.1 | custom fusion | bytes 90112 | tf_op jit(solution)/shard_map/gather | solution.py:18
  241.5 0.3 copy.13
  241.9 0.0 copy-done.1
  241.9 0.0 copy-done.4
  241.9 0.0 copy-done.5
  241.9 1.3 multiply_reduce_fusion
  243.2 1.1 fusion.9
  244.3 1.3 fusion.1
  245.6 0.0 reduce-scatter.3.cloned.1.call-update
  245.6 0.0 reduce-scatter.5.cloned.1.call-start
  245.7 0.4 copy.20
  246.1 21.2 %broadcast_in_dim.20 = f32[131072,5]{1,0:T(8,128)} broadcast(f32[]{:T(128)} %constant.0.clone.1), dimensions={} | broadcast | bytes 2621444 | tf_op jit(solution)/shard_map/broadcast_in_dim | solution.py:26
  267.2 201.5 %scatter_fusion = f32[131072,5]{1,0:T(8,128)} fusion(f32[131072,5]{1,0:T(8,128)} %broadcast_in_dim.20, s32[2048]{0:T(1024)S(1)} %bitcast.30, f32[2048,5]{1,0:T(8,128)S(1)} %bitcast.26), kind=kCustom, calls=%fused_computation.2 | custom fusion | flops 10240 | bytes 131072 | tf_op jit(solution)/shard_map/scatter-add | solution.py:26
  468.7 0.0 reduce-scatter.5.cloned.1.call-update
  468.8 75.8 %psum.15 = f32[]{:T(128)} all-reduce(f32[]{:T(128)} %get-tuple-element.8), channel_id=1, replica_groups=mesh['sky'=8,'tm'=32] {'sky','tm'}, use_global_device_ids=true, to_apply=%region_6.7 | all-reduce | flops 1 | bytes 8 | tf_op jit(solution)/shard_map/psum | solution.py:23
  544.6 0.0 reduce-scatter.3.cloned.1.call-done
  544.6 23.4 %psum.14 = f32[16,256]{1,0:T(8,128)} all-reduce(f32[16,256]{1,0:T(8,128)} %reduce-scatter.3.cloned.1.call-done), channel_id=1, replica_groups=mesh['sky'=8,'tm'=32] {'sky'}, use_global_device_ids=true, to_apply=%region_2.3 | all-reduce | flops 4096 | bytes 32768 | tf_op jit(solution)/shard_map/psum | solution.py:35
  568.0 200.2 %reduce-scatter.5.cloned.1.call-done = f32[5,4096]{0,1:T(8,128)} async-done(((f32[5,131072]{0,1:T(8,128)}), f32[5,4096]{0,1:T(8,128)}) %reduce-scatter.5.cloned.1.call-update) | async-done | bytes 81936 | tf_op jit(solution)/shard_map/reduce_scatter | solution.py:27
  768.3 2.9 copy.15
  (5 shorter events, 0.0 us)
Async XLA Ops:
  7.2 30.5 %copy-start = (f32[16,128,256]{2,1,0:T(8,128)S(1)}, f32[16,128,256]{2,1,0:T(8,128)}, u32[]{:S(2)}) copy-start(f32[16,128,256]{2,1,0:T(8,128)} %param.8) | copy-start | bytes 6291460
  7.2 3.2 copy-start.6
  7.2 3.2 copy-start.3
  7.2 30.4 %copy-start.2 = (s32[16,128]{1,0:T(8,128)S(1)}, s32[16,128]{1,0:T(8,128)}, u32[]{:S(2)}) copy-start(s32[16,128]{1,0:T(8,128)} %param.11) | copy-start | bytes 24580
  7.2 213.9 %all-gather.2.cloned.1.call-start = ((), (), s32[]{:S(2)}) async-start(), calls=%async_computation.2 | async-start | bytes 69206016 | tf_op jit(solution)/shard_map/all_gather | solution.py:13
  10.3 534.3 %reduce-scatter.3.cloned.1.call-start = ((), (), s32[]{:S(2)}) async-start(), calls=%async_computation.3 | async-start | bytes 540672 | tf_op jit(solution)/shard_map/reduce_scatter | solution.py:34
  10.4 231.5 %copy-start.1 = (f32[5,16,128]{2,1,0:T(8,128)S(1)}, f32[5,16,128]{2,1,0:T(8,128)}, u32[]{:S(2)}) copy-start(f32[5,16,128]{2,1,0:T(8,128)} %param.12) | copy-start | bytes 122884
  10.4 231.5 %copy-start.4 = (f32[16,128]{1,0:T(8,128)S(1)}, f32[16,128]{1,0:T(8,128)}, u32[]{:S(2)}) copy-start(f32[16,128]{1,0:T(8,128)} %param.13) | copy-start | bytes 24580
  10.4 231.5 %copy-start.5 = (s32[16]{0:T(128)S(1)}, s32[16]{0:T(128)}, u32[]{:S(2)}) copy-start(s32[16]{0:T(128)} %param.10) | copy-start | bytes 196
  245.6 522.6 %reduce-scatter.5.cloned.1.call-start = ((), (), s32[]{:S(2)}) async-start(), calls=%async_computation.4 | async-start | bytes 69206016 | tf_op jit(solution)/shard_map/reduce_scatter | solution.py:27
Sparse Core Ops, SparseCore 0:
  10.6 210.4 all-gather.1
  245.8 81.6 reduce-scatter.2
  468.9 299.3 reduce-scatter.4
where the time goes:
time: 785 us; the launch traced here: 778 us
  waiting for transfers between devices  382 us (49%)
  other arithmetic  203 us (26%)
  blocking collectives  126 us (16%)
  local copies, waits for them, and re-layouts  48.8 us (6%)
  between operations  13.9 us (2%)
    scatter-add x1, other arithmetic, per_device(): jax.ops.segment_sum(terms.T, src_index.reshape(-1), num_segments=region_s...  202 us
    reduce_scatter x1, waiting for transfers between devices, per_device(): lax.psum_scatter(src_terms, 'tm', scatter_dimension=1, tiled=True)  200 us
    all_gather x1, waiting for transfers between devices, per_device(): src_region = lax.all_gather(src_dir, 'tm', axis=1, tiled=True)  182 us
    psum x1, blocking collectives, per_device(): curvature = lax.psum(jnp.sum(projected * weighted), ('sky', 'tm'))  75.8 us
    all_gather x1, blocking collectives, per_device(): att_whole = lax.all_gather(att_dir, 'tm', axis=0, tiled=True)  26.6 us
    psum x1, blocking collectives, per_device(): att_normal = lax.psum(owned, 'sky')  23.4 us
    broadcast_in_dim x1, local copies, waits for them, and re-layouts, per_device(): jax.ops.segment_sum(terms.T, src_index.reshape(-1), num_segments=region_s...  21.2 us
    gather x2, local copies, waits for them, and re-layouts, per_device(): picked = src_region[:, src_index]  20.8 us
  transfers between devices with their start and end apart: 3, of which 2 were waited for; matrix products, arithmetic and copies ran while one was open for 29% of the time, Pallas kernels for 0%

commit v1 on v0

v1 whole, which is shorter than its diff:
```python
import functools

import jax
import jax.numpy as jnp
from jax import lax
from jax.experimental import pallas as pl
from jax.experimental.pallas import tpu as pltpu
from jax.sharding import PartitionSpec as P

LANES = 128
ROWS_MSG = 8
SLOT_T = 2
F32, BF16, I32 = jnp.float32, jnp.bfloat16, jnp.int32
NT = (((1,), (1,)), ((), ()))
TN = (((0,), (0,)), ((), ()))


def halves(x):
    hi = x.astype(BF16)
    return hi, (x - hi.astype(F32)).astype(BF16)


def iota(shape, dim):
    return lax.broadcasted_iota(I32, shape, dim)


def lanes_of(row, index):
    return jnp.take_along_axis(jnp.broadcast_to(row, index.shape), index, axis=1)


def kernel(
    n_sky, n_tm,
    seg_ref, cnt_ref, tiles_hbm, idx_hbm, coef_hbm, wgt_hbm, att_hbm, src_hbm,
    proj_o, att_o, src_o, curv_o,
    tiles_v, idx_v, coef_v, wgt_v, att_v, src_v, thi, tlo, low_v, dir_v, rank_v, inv_v,
    s1, r1, s2, r2, s3, r3, sz, rz,
    in_sem, send_sem, recv_sem,
):
    params, td, _ = coef_v.shape
    seg_dev, cols = att_v.shape
    src_dev = src_v.shape[1]
    nb = n_tm
    chunks = src_dev // LANES
    half = cols // LANES
    me, z = lax.axis_index("tm"), lax.axis_index("sky")

    loads = [
        pltpu.make_async_copy(a, b, in_sem.at[i])
        for i, (a, b) in enumerate(
            ((idx_hbm, idx_v), (coef_hbm, coef_v), (src_hbm, src_v), (att_hbm, att_v),
             (wgt_hbm, wgt_v), (tiles_hbm, tiles_v))
        )
    ]
    for copy in loads:
        copy.start()

    barrier = pltpu.get_barrier_semaphore()

    @pl.loop(1, n_tm)
    def _(i):
        pl.semaphore_signal(barrier, 1, device_id=(z, lax.rem(me + i, n_tm)))

    @pl.loop(1, n_sky)
    def _(i):
        pl.semaphore_signal(barrier, 1, device_id=(lax.rem(z + i, n_sky), me))

    def strided(ref, row):
        return ref[pl.ds(row, nb, stride=ROWS_MSG), :]

    def put(ref, row, value):
        ref[pl.ds(row, nb, stride=ROWS_MSG), :] = value

    def block(q):
        return pl.ds(pl.multiple_of(q * ROWS_MSG, ROWS_MSG), ROWS_MSG)

    def exchange(src, dst, k):
        @pl.loop(1, n_tm)
        def _(i):
            q = lax.rem(me + i, n_tm)
            pltpu.make_async_remote_copy(
                src_ref=src.at[block(q)], dst_ref=dst.at[block(me)],
                send_sem=send_sem.at[k], recv_sem=recv_sem.at[k],
                device_id=(z, q), device_id_type=pl.DeviceIdType.MESH,
            ).start()

        dst[block(me), :] = src[block(me), :]

    def await_bytes(ref, rows, sem):
        view = ref.at[pl.ds(0, rows)]
        pltpu.make_async_copy(view, view, sem).wait()

    seg_shift = seg_dev.bit_length() - 1
    owner_t = [seg_ref[t] >> seg_shift for t in range(td)]
    local_t = [seg_ref[t] & (seg_dev - 1) for t in range(td)]
    rank_t = []
    for t in range(td):
        r = jnp.int32(0)
        for before in range(t):
            r = r + (owner_t[before] == owner_t[t]).astype(I32)
        rank_t.append(r)
    bins, lane = iota((nb, LANES), 0), iota((nb, LANES), 1)
    wanted = jnp.zeros((nb, LANES), I32)
    for t in range(td):
        hit = (bins == owner_t[t]) & (lane == rank_t[t])
        wanted = jnp.where(hit, local_t[t] + 1, wanted)

    loads[0].wait()
    src_shift = src_dev.bit_length() - 1
    idx = idx_v[...]
    owner = idx >> src_shift
    mine = [jnp.broadcast_to(owner[t : t + 1], (nb, LANES)) == bins for t in range(td)]
    ones = [m.astype(F32) for m in mine]
    i0, i1 = iota((LANES, 2 * LANES), 0), iota((LANES, 2 * LANES), 1)
    tri = ((i0 < i1) | (i1 >= LANES)).astype(F32).astype(BF16)
    counts = jnp.dot(
        jnp.concatenate(ones, axis=0).astype(BF16), tri, preferred_element_type=F32
    )
    offset = jnp.zeros((nb, LANES), F32)
    slot_id = iota((LANES, LANES), 0)
    spots, origin = [], []
    lane_f = lane.astype(F32)
    for t in range(td):
        here = counts[t * nb : (t + 1) * nb]
        rank = jnp.sum(jnp.where(mine[t], here[:, :LANES] + offset, 0.0), axis=0, keepdims=True)
        rank = rank.astype(I32)
        offset = offset + here[:, LANES:]
        rank_v[t : t + 1, :] = rank
        spots.append((jnp.broadcast_to(rank, (LANES, LANES)) == slot_id).astype(F32).astype(BF16))
        origin.append(jnp.concatenate([ones[t] * (t + 1.0), ones[t] * lane_f], axis=0).astype(BF16))
    found = lax.dot_general(
        jnp.concatenate(origin, axis=1), jnp.concatenate(spots, axis=1), NT,
        preferred_element_type=F32,
    ).astype(I32)
    inv_v[...] = found

    def to_slots(rows):
        tile, col = inv_v[:nb, :], inv_v[nb:, :]
        out = jnp.zeros((nb, LANES), F32)
        for t in range(td):
            out = jnp.where(tile == t + 1, lanes_of(rows[t : t + 1], col), out)
        return out

    loads[1].wait()
    for k in range(params):
        put(s1, k, to_slots(coef_v[k]))
    put(s1, params, to_slots((idx & (src_dev - 1)).astype(F32)))
    put(s1, params + 1, wanted.astype(F32))
    put(s1, params + 2, jnp.zeros((nb, LANES), F32))

    pl.semaphore_wait(barrier, n_tm + n_sky - 2)
    exchange(s1, r1, 0)

    loads[5].wait()

    @pl.loop(0, td)
    def _(t):
        rows = pl.ds(pl.multiple_of(t * LANES, LANES), LANES)
        hi, lo = halves(tiles_v[t])
        thi[rows, :] = hi
        tlo[rows, :] = lo

    for copy in (loads[2], loads[3], loads[4]):
        copy.wait()

    await_bytes(r1, (n_tm - 1) * ROWS_MSG, recv_sem.at[0])

    asked = strided(r1, params).astype(I32)
    chunk, col = asked >> 7, asked & (LANES - 1)
    picked = [jnp.zeros((nb, LANES), F32) for _ in range(params)]
    for h in range(chunks):
        here = chunk == h
        for k in range(params):
            row = src_v[k : k + 1, h * LANES : (h + 1) * LANES]
            picked[k] = jnp.where(here, lanes_of(row, col), picked[k])
    total = jnp.zeros((nb, LANES), F32)
    for k in range(params):
        total = total + strided(r1, k) * picked[k]
    put(s2, 0, total)
    segs = strided(r1, params + 1).astype(I32)
    seg_id = iota((nb, seg_dev), 1) + 1
    att_pair = jnp.concatenate(halves(att_v[...]), axis=1)
    choice = []
    for r in range(SLOT_T):
        pick = jnp.broadcast_to(segs[:, r : r + 1], (nb, seg_dev)) == seg_id
        choice.append(pick.astype(F32).astype(BF16))
        both = jnp.dot(choice[r], att_pair, preferred_element_type=F32)
        rows = both[:, :cols] + both[:, cols:]
        for c in range(half):
            put(s2, 1 + r * half + c, rows[:, c * LANES : (c + 1) * LANES])
    for k in range(1 + SLOT_T * half, ROWS_MSG):
        put(s2, k, jnp.zeros((nb, LANES), F32))
    exchange(s2, r2, 1)

    for p in range(nb):
        low_v[:, p * LANES : (p + 1) * LANES] = (
            jnp.broadcast_to(col[p : p + 1], (LANES, LANES)) == slot_id
        ).astype(F32).astype(BF16)
    obs_t, obs_row = iota((td, LANES), 0), iota((td, LANES), 1)
    count = jnp.zeros((td, LANES), I32)
    for t in range(td):
        count = jnp.where(obs_t == t, cnt_ref[t], count)
    live = obs_row < count

    await_bytes(r2, (n_tm - 1) * ROWS_MSG, recv_sem.at[1])

    for t in range(td):
        for c in range(half):
            dir_v[t : t + 1, c * LANES : (c + 1) * LANES] = r2[
                pl.ds(owner_t[t] * ROWS_MSG + 1 + rank_t[t] * half + c, 1), :
            ]
    dir_hi, dir_lo = halves(dir_v[...])
    first = lax.dot_general(
        jnp.concatenate([dir_hi, dir_lo], axis=0), thi[...], NT, preferred_element_type=F32
    )
    second = lax.dot_general(dir_hi, tlo[...], NT, preferred_element_type=F32)
    sums = first[:td] + first[td:] + second
    part = jnp.zeros((td, LANES), F32)
    for t in range(td):
        part = jnp.where(obs_t == t, sums[:, t * LANES : (t + 1) * LANES], part)
    answers = strided(r2, 0)
    rank = rank_v[...]
    source = jnp.zeros((td, LANES), F32)
    for b in range(nb):
        source = jnp.where(owner == b, lanes_of(answers[b : b + 1], rank), source)
    projected = jnp.where(live, part + source, 0.0)
    proj_o[...] = projected
    weighted = wgt_v[...] * projected
    curvature = jnp.sum(projected * weighted)

    put(s3, 0, to_slots(weighted))
    w_hi, w_lo = halves(weighted)
    w_hi, w_lo = w_hi.astype(F32), w_lo.astype(F32)
    slots = iota((SLOT_T * nb, LANES), 0)
    left = []
    for t in range(td):
        here = slots == rank_t[t] * nb + owner_t[t]
        left.append(
            jnp.concatenate(
                [
                    jnp.where(here, jnp.broadcast_to(w[t : t + 1], slots.shape), 0.0)
                    for w in (w_hi, w_lo)
                ],
                axis=0,
            ).astype(BF16)
        )
    left = jnp.concatenate(left, axis=1)
    n_slots = SLOT_T * nb
    grad = jnp.dot(left, thi[...], preferred_element_type=F32)
    grad = (
        grad[:n_slots]
        + grad[n_slots:]
        + jnp.dot(left[:n_slots], tlo[...], preferred_element_type=F32)
    )
    for r in range(SLOT_T):
        for c in range(half):
            put(
                s3, 1 + r * half + c,
                grad[r * nb : (r + 1) * nb, c * LANES : (c + 1) * LANES],
            )
    put(s3, 1 + SLOT_T * half, jnp.full((nb, LANES), curvature, F32))
    for k in range(2 + SLOT_T * half, ROWS_MSG):
        put(s3, k, jnp.zeros((nb, LANES), F32))
    exchange(s3, r3, 2)
    await_bytes(r3, (n_tm - 1) * ROWS_MSG, recv_sem.at[2])

    zrows = seg_dev * half + 8

    def zblock(q):
        return pl.ds(pl.multiple_of(q * zrows, 8), zrows)

    owned = jnp.zeros((seg_dev, cols), F32)
    for r in range(SLOT_T):
        rows = jnp.concatenate([strided(r3, 1 + r * half + c) for c in range(half)], axis=1)
        both = lax.dot_general(
            choice[r], jnp.concatenate(halves(rows), axis=1), TN, preferred_element_type=F32
        )
        owned = owned + both[:, :cols] + both[:, cols:]
    for c in range(half):
        sz[c * seg_dev : (c + 1) * seg_dev, :] = owned[:, c * LANES : (c + 1) * LANES]
    curv_rows = jnp.sum(strided(r3, 1 + SLOT_T * half), axis=0, keepdims=True)
    sz[seg_dev * half : zrows, :] = jnp.broadcast_to(curv_rows, (8, LANES))

    @pl.loop(1, n_sky)
    def _(i):
        q = lax.rem(z + i, n_sky)
        pltpu.make_async_remote_copy(
            src_ref=sz, dst_ref=rz.at[zblock(z)],
            send_sem=send_sem.at[3], recv_sem=recv_sem.at[3],
            device_id=(q, me), device_id_type=pl.DeviceIdType.MESH,
        ).start()

    rz[zblock(z), :] = sz[...]

    back = strided(r3, 0)
    chunk_id = iota((chunks, LANES), 0)
    terms = []
    for k in range(params):
        hi, lo = halves(strided(r1, k) * back)
        terms.append((hi.astype(F32), lo.astype(F32)))
    grid = []
    for p in range(nb):
        here = jnp.broadcast_to(chunk[p : p + 1], chunk_id.shape) == chunk_id
        grid.append(
            jnp.concatenate(
                [
                    jnp.where(here, jnp.broadcast_to(terms[k][i][p : p + 1], here.shape), 0.0)
                    for i in range(2)
                    for k in range(params)
                ],
                axis=0,
            ).astype(BF16)
        )
    both = lax.dot_general(
        jnp.concatenate(grid, axis=1), low_v[...], NT, preferred_element_type=F32
    )
    rows = params * chunks
    spread = both[:rows] + both[rows:]
    for k in range(params):
        for h in range(chunks):
            src_o[k : k + 1, h * LANES : (h + 1) * LANES] = spread[
                k * chunks + h : k * chunks + h + 1
            ]

    await_bytes(rz, (n_sky - 1) * zrows, recv_sem.at[3])
    summed = rz[0:zrows, :]
    for q in range(1, n_sky):
        summed = summed + rz[q * zrows : (q + 1) * zrows, :]
    for c in range(half):
        att_o[:, c * LANES : (c + 1) * LANES] = summed[c * seg_dev : (c + 1) * seg_dev]
    curv_o[0] = summed[seg_dev * half, 0]

    for k, ref in enumerate((s1, s2, s3)):
        await_bytes(ref, (n_tm - 1) * ROWS_MSG, send_sem.at[k])
    await_bytes(rz, (n_sky - 1) * zrows, send_sem.at[3])


def per_device(n_sky, n_tm, tiles, tile_seg, tile_count, src_index, src_coef, obs_weight, att_dir, src_dir):
    td, rows, cols = tiles.shape
    params, src_dev = src_dir.shape
    seg_dev = att_dir.shape[0]
    msg = pltpu.VMEM((n_tm * ROWS_MSG, LANES), F32)
    zrows = seg_dev * (cols // LANES) + 8
    vmem, smem, hbm = (
        pl.BlockSpec(memory_space=s) for s in (pltpu.VMEM, pltpu.SMEM, pl.ANY)
    )
    projected, att_normal, src_normal, curvature = pl.pallas_call(
        functools.partial(kernel, n_sky, n_tm),
        out_shape=(
            jax.ShapeDtypeStruct((td, rows), F32),
            jax.ShapeDtypeStruct((seg_dev, cols), F32),
            jax.ShapeDtypeStruct((params, src_dev), F32),
            jax.ShapeDtypeStruct((1,), F32),
        ),
        in_specs=[smem, smem, hbm, hbm, hbm, hbm, hbm, hbm],
        out_specs=(vmem, vmem, vmem, smem),
        scratch_shapes=[
            pltpu.VMEM((td, rows, cols), F32),
            pltpu.VMEM((td, rows), I32),
            pltpu.VMEM((params, td, rows), F32),
            pltpu.VMEM((td, rows), F32),
            pltpu.VMEM((seg_dev, cols), F32),
            pltpu.VMEM((params, src_dev), F32),
            pltpu.VMEM((td * rows, cols), BF16),
            pltpu.VMEM((td * rows, cols), BF16),
            pltpu.VMEM((LANES, n_tm * LANES), BF16),
            pltpu.VMEM((td, cols), F32),
            pltpu.VMEM((td, rows), I32),
            pltpu.VMEM((2 * n_tm, LANES), I32),
            msg, msg, msg, msg, msg, msg,
            pltpu.VMEM((zrows, LANES), F32),
            pltpu.VMEM((n_sky * zrows, LANES), F32),
            pltpu.SemaphoreType.DMA((6,)),
            pltpu.SemaphoreType.DMA((4,)),
            pltpu.SemaphoreType.DMA((4,)),
        ],
        compiler_params=pltpu.CompilerParams(
            collective_id=0, has_side_effects=True, vmem_limit_bytes=48 << 20
        ),
    )(tile_seg, tile_count, tiles, src_index, src_coef, obs_weight, att_dir, src_dir)
    return projected, att_normal, src_normal, curvature.reshape(())


def solution(mesh):
    placed = (
        P(("sky", "tm"), None, None),
        P(("sky", "tm")),
        P(("sky", "tm")),
        P(("sky", "tm"), None),
        P(None, ("sky", "tm"), None),
        P(("sky", "tm"), None),
        P("tm", None),
        P(None, ("sky", "tm")),
    )
    return jax.shard_map(
        functools.partial(per_device, mesh.shape["sky"], mesh.shape["tm"]),
        mesh=mesh,
        in_specs=placed,
        out_specs=(P(("sky", "tm"), None), P("tm", None), P(None, ("sky", "tm")), P()),
        check_vma=False,
    )
```

time: 785 us -> 48 us (0.06)
  waiting for transfers between devices: 382 us -> 0 us
  other arithmetic: 203 us -> 0 us
  blocking collectives: 126 us -> 0 us
  local copies, waits for them, and re-layouts: 48.8 us -> 8.55 us
  Pallas kernels: 0 us -> 36.6 us
  between operations: 13.9 us -> 2.47 us
    scatter-add x1 -> x0, other arithmetic: 202 us -> none  [per_device(): jax.ops.segment_sum(terms.T, src_index.reshape(-1), num_segments=region_s...]
    reduce_scatter x2 -> x0, waiting for transfers between devices: 200 us -> none  [the longest x1 200 us: per_device(): lax.psum_scatter(src_terms, 'tm', scatter_dimension=1, tiled=True)]
    all_gather x1 -> x0, waiting for transfers between devices: 182 us -> none  [per_device(): src_region = lax.all_gather(src_dir, 'tm', axis=1, tiled=True)]
    psum x2 -> x0, blocking collectives: 99.3 us -> none  [the longest x1 75.8 us: per_device(): curvature = lax.psum(jnp.sum(projected * weighted), ('sky', 'tm'))]
    pallas_call x0 -> x1, Pallas kernels: none -> 36.6 us  [per_device(): pl.pallas_call(functools.partial(kernel, n_sky, n_tm), out_shape=(jax.Sha...]
    all_gather x1 -> x0, blocking collectives: 26.6 us -> none  [per_device(): att_whole = lax.all_gather(att_dir, 'tm', axis=0, tiled=True)]
    gather x3 -> x0, local copies, waits for them, and re-layouts: 21.3 us -> none  [the longest x2 20.8 us: per_device(): picked = src_region[:, src_index]]
    broadcast_in_dim x1 -> x0, local copies, waits for them, and re-layouts: 21.2 us -> none  [per_device(): jax.ops.segment_sum(terms.T, src_index.reshape(-1), num_segments=region_s...]
  transfers between devices with their start and end apart: 3 -> 0, of which waited for: 2 -> 0; matrix products, arithmetic and copies ran while one was open for 29% -> 0% of each run, Pallas kernels for 0% -> 0%
where the time goes in v1:
time: 48 us; the launch traced here: 47.6 us
  Pallas kernels  36.6 us (76%)
  local copies, waits for them, and re-layouts  8.55 us (18%)
  between operations  2.47 us (5%)
    pallas_call x1, Pallas kernels, per_device(): pl.pallas_call(functools.partial(kernel, n_sky, n_tm), out_shape=(jax.Sha...  36.6 us
    unnamed x19, local copies, waits for them, and re-layouts  8.55 us

profile of v1, /device:TPU:1, one launch (start us, length us, event | category | flops | bytes accessed | tf_op | source)
XLA Modules:
  0.0 47.6 jit_solution(13479292994471246674)
XLA Ops:
  0.6 0.0 copy-start
  0.6 1.6 %copy-done = f32[16,128,256]{2,1,0:T(8,128)S(1)} copy-done((f32[16,128,256]{2,1,0:T(8,128)S(1)}, f32[16,128,256]{2,1,0:T(8,128)}, u32[]{:S(2)}) %copy-start) | copy-done | bytes 2097176
  2.2 0.0 copy-start.1
  2.2 0.9 %copy-done.1 = f32[5,4096]{1,0:T(8,128)S(1)} copy-done((f32[5,4096]{1,0:T(8,128)S(1)}, f32[5,4096]{1,0:T(8,128)}, u32[]{:S(2)}) %copy-start.1) | copy-done | bytes 81944
  3.1 0.0 copy-start.2
  3.1 0.8 %copy-done.2 = f32[5,16,128]{2,1,0:T(8,128)S(1)} copy-done((f32[5,16,128]{2,1,0:T(8,128)S(1)}, f32[5,16,128]{2,1,0:T(8,128)}, u32[]{:S(2)}) %copy-start.2) | copy-done | bytes 40984
  3.9 0.0 copy-start.3
  3.9 0.7 %copy-done.3 = f32[16,256]{1,0:T(8,128)S(1)} copy-done((f32[16,256]{1,0:T(8,128)S(1)}, f32[16,256]{1,0:T(8,128)}, u32[]{:S(2)}) %copy-start.3) | copy-done | bytes 16408
  4.6 0.0 copy-start.4
  4.6 0.7 %copy-done.4 = s32[16,128]{1,0:T(8,128)S(1)} copy-done((s32[16,128]{1,0:T(8,128)S(1)}, s32[16,128]{1,0:T(8,128)}, u32[]{:S(2)}) %copy-start.4) | copy-done | bytes 8216
  5.3 0.0 copy-start.5
  5.3 0.7 %copy-done.5 = f32[16,128]{1,0:T(8,128)S(1)} copy-done((f32[16,128]{1,0:T(8,128)S(1)}, f32[16,128]{1,0:T(8,128)}, u32[]{:S(2)}) %copy-start.5) | copy-done | bytes 8216
  6.0 0.0 copy-start.6
  6.0 0.7 %copy-done.6 = s32[16]{0:T(128)S(1)} copy-done((s32[16]{0:T(128)S(1)}, s32[16]{0:T(128)}, u32[]{:S(2)}) %copy-start.6) | copy-done | bytes 88
  6.7 0.0 copy-start.7
  6.7 0.7 %copy-done.7 = s32[16]{0:T(128)S(1)} copy-done((s32[16]{0:T(128)S(1)}, s32[16]{0:T(128)}, u32[]{:S(2)}) %copy-start.7) | copy-done | bytes 88
  7.3 36.6 %shard_map.111 = (f32[16,128]{1,0:T(8,128)S(1)}, f32[16,256]{1,0:T(8,128)S(1)}, f32[5,4096]{1,0:T(8,128)S(1)}, f32[1]{0:T(128)}) custom-call(s32[16]{0:T(128)S(1)} %copy-done.6, s32[16]{0:T(128)S(1)} %copy-done.7, f32[16,128,256]{2,1,0:T(8,128)S(1)} %copy-done, s32[16,128]{1,0:T(8,128)S(1)} %copy-done.4, f32[5,16,128]{2,1,0:T(8,128)S(1)} %copy-done.2, ...), custom_call_target="tpu_custom_call" | custom-call | tf_op jit(solution)/shard_map/pallas_call | solution.py:346
  43.9 0.6 %copy.16 = f32[16,128]{1,0:T(8,128)} copy(f32[16,128]{1,0:T(8,128)S(1)} %get-tuple-element.16) | data formatting | bytes 16384
  44.5 0.6 %copy.17 = f32[16,256]{1,0:T(8,128)} copy(f32[16,256]{1,0:T(8,128)S(1)} %get-tuple-element.17) | data formatting | bytes 32768
  45.1 0.7 %copy.18 = f32[5,4096]{1,0:T(8,128)} copy(f32[5,4096]{1,0:T(8,128)S(1)} %get-tuple-element.18) | data formatting | bytes 163840
Async XLA Ops:
  0.6 1.6 %copy-start = (f32[16,128,256]{2,1,0:T(8,128)S(1)}, f32[16,128,256]{2,1,0:T(8,128)}, u32[]{:S(2)}) copy-start(f32[16,128,256]{2,1,0:T(8,128)} %tiles_hbm.1) | copy-start | bytes 6291460
  2.2 0.9 %copy-start.1 = (f32[5,4096]{1,0:T(8,128)S(1)}, f32[5,4096]{1,0:T(8,128)}, u32[]{:S(2)}) copy-start(f32[5,4096]{1,0:T(8,128)} %src_hbm.1) | copy-start | bytes 245764
  3.1 0.8 %copy-start.2 = (f32[5,16,128]{2,1,0:T(8,128)S(1)}, f32[5,16,128]{2,1,0:T(8,128)}, u32[]{:S(2)}) copy-start(f32[5,16,128]{2,1,0:T(8,128)} %coef_hbm.1) | copy-start | bytes 122884
  3.9 0.7 %copy-start.3 = (f32[16,256]{1,0:T(8,128)S(1)}, f32[16,256]{1,0:T(8,128)}, u32[]{:S(2)}) copy-start(f32[16,256]{1,0:T(8,128)} %att_hbm.1) | copy-start | bytes 49156
  4.6 0.7 %copy-start.4 = (s32[16,128]{1,0:T(8,128)S(1)}, s32[16,128]{1,0:T(8,128)}, u32[]{:S(2)}) copy-start(s32[16,128]{1,0:T(8,128)} %idx_hbm.1) | copy-start | bytes 24580
  5.3 0.7 %copy-start.5 = (f32[16,128]{1,0:T(8,128)S(1)}, f32[16,128]{1,0:T(8,128)}, u32[]{:S(2)}) copy-start(f32[16,128]{1,0:T(8,128)} %wgt_hbm.1) | copy-start | bytes 24580
  6.0 0.7 %copy-start.6 = (s32[16]{0:T(128)S(1)}, s32[16]{0:T(128)}, u32[]{:S(2)}) copy-start(s32[16]{0:T(128)} %seg_ref.1) | copy-start | bytes 196
  6.7 0.7 %copy-start.7 = (s32[16]{0:T(128)S(1)}, s32[16]{0:T(128)}, u32[]{:S(2)}) copy-start(s32[16]{0:T(128)} %cnt_ref.1) | copy-start | bytes 196

commit v2 on v1

--- a/solution.py
+++ b/solution.py
@@ -9,6 +9,8 @@
 
 LANES = 128
 ROWS_MSG = 8
+GROUP = 8
+SCOPED = 58 << 20
 SLOT_T = 2
 F32, BF16, I32 = jnp.float32, jnp.bfloat16, jnp.int32
 NT = (((1,), (1,)), ((), ()))
@@ -28,21 +30,34 @@
     return jnp.take_along_axis(jnp.broadcast_to(row, index.shape), index, axis=1)
 
 
+def hops(step, extents):
+    total = 0
+    for n in reversed(extents):
+        part = step % n
+        step //= n
+        total += min(part, n - part)
+    return total
+
+
 def kernel(
     n_sky, n_tm,
     seg_ref, cnt_ref, tiles_hbm, idx_hbm, coef_hbm, wgt_hbm, att_hbm, src_hbm,
-    proj_o, att_o, src_o, curv_o,
+    proj_o, sums_o, src_o,
     tiles_v, idx_v, coef_v, wgt_v, att_v, src_v, thi, tlo, low_v, dir_v, rank_v, inv_v,
     s1, r1, s2, r2, s3, r3, sz, rz,
-    in_sem, send_sem, recv_sem,
+    in_sem, send_sem, recv_sem, zsend_sem, zrecv_sem,
 ):
     params, td, _ = coef_v.shape
     seg_dev, cols = att_v.shape
     src_dev = src_v.shape[1]
     nb = n_tm
+    groups = n_tm // GROUP
     chunks = src_dev // LANES
     half = cols // LANES
     me, z = lax.axis_index("tm"), lax.axis_index("sky")
+    my_group = me // GROUP
+    across = sorted(range(groups), key=lambda k: -min(k, groups - k))
+    within = sorted(range(GROUP), key=lambda k: -hops(k, (4, 2)))
 
     loads = [
         pltpu.make_async_copy(a, b, in_sem.at[i])
@@ -58,7 +73,7 @@
 
     @pl.loop(1, n_tm)
     def _(i):
-        pl.semaphore_signal(barrier, 1, device_id=(z, lax.rem(me + i, n_tm)))
+        pl.semaphore_signal(barrier, 1, device_id=(z, jnp.bitwise_xor(me, i)))
 
     @pl.loop(1, n_sky)
     def _(i):
@@ -70,24 +85,39 @@
     def put(ref, row, value):
         ref[pl.ds(row, nb, stride=ROWS_MSG), :] = value
 
-    def block(q):
-        return pl.ds(pl.multiple_of(q * ROWS_MSG, ROWS_MSG), ROWS_MSG)
-
-    def exchange(src, dst, k):
-        @pl.loop(1, n_tm)
-        def _(i):
-            q = lax.rem(me + i, n_tm)
+    def group_start(k):
+        return pl.multiple_of(jnp.bitwise_xor(my_group, k) * (GROUP * ROWS_MSG), GROUP * ROWS_MSG)
+
+    def strided_group(ref, row, k):
+        return ref[pl.ds(group_start(k) + row, GROUP, stride=ROWS_MSG), :]
+
+    def put_group(ref, row, k, value):
+        ref[pl.ds(group_start(k) + row, GROUP, stride=ROWS_MSG), :] = value
+
+    def block(q, first, rows):
+        return pl.ds(pl.multiple_of(q * ROWS_MSG, ROWS_MSG) + first, rows)
+
+    def send_group(src, dst, phase, k, first, rows):
+        for j in within:
+            step = k * GROUP + j
+            if step == 0:
+                continue
+            q = jnp.bitwise_xor(me, step)
             pltpu.make_async_remote_copy(
-                src_ref=src.at[block(q)], dst_ref=dst.at[block(me)],
-                send_sem=send_sem.at[k], recv_sem=recv_sem.at[k],
+                src_ref=src.at[block(q, first, rows)], dst_ref=dst.at[block(me, first, rows)],
+                send_sem=send_sem.at[phase], recv_sem=recv_sem.at[phase, k],
                 device_id=(z, q), device_id_type=pl.DeviceIdType.MESH,
             ).start()
 
-        dst[block(me), :] = src[block(me), :]
+    def keep(src, dst):
+        dst[block(me, 0, ROWS_MSG), :] = src[block(me, 0, ROWS_MSG), :]
 
     def await_bytes(ref, rows, sem):
         view = ref.at[pl.ds(0, rows)]
         pltpu.make_async_copy(view, view, sem).wait()
+
+    def await_group(ref, phase, k, rows):
+        await_bytes(ref, (GROUP - (k == 0)) * rows, recv_sem.at[phase, k])
 
     seg_shift = seg_dev.bit_length() - 1
     owner_t = [seg_ref[t] >> seg_shift for t in range(td)]
@@ -103,6 +133,7 @@
     for t in range(td):
         hit = (bins == owner_t[t]) & (lane == rank_t[t])
         wanted = jnp.where(hit, local_t[t] + 1, wanted)
+    put(s1, params + 1, wanted.astype(F32))
 
     loads[0].wait()
     src_shift = src_dev.bit_length() - 1
@@ -144,11 +175,12 @@
     for k in range(params):
         put(s1, k, to_slots(coef_v[k]))
     put(s1, params, to_slots((idx & (src_dev - 1)).astype(F32)))
-    put(s1, params + 1, wanted.astype(F32))
-    put(s1, params + 2, jnp.zeros((nb, LANES), F32))
-
+
+    asked_rows = params + 2
     pl.semaphore_wait(barrier, n_tm + n_sky - 2)
-    exchange(s1, r1, 0)
+    for k in across:
+        send_group(s1, r1, 0, k, 0, asked_rows)
+    keep(s1, r1)
 
     loads[5].wait()
 
@@ -161,48 +193,71 @@
 
     for copy in (loads[2], loads[3], loads[4]):
         copy.wait()
-
-    await_bytes(r1, (n_tm - 1) * ROWS_MSG, recv_sem.at[0])
+    att_pair = jnp.concatenate(halves(att_v[...]), axis=1)
+    obs_t, obs_row = iota((td, LANES), 0), iota((td, LANES), 1)
+    count = jnp.zeros((td, LANES), I32)
+    for t in range(td):
+        count = jnp.where(obs_t == t, cnt_ref[t], count)
+    live = obs_row < count
+
+    answer_rows = 1 + SLOT_T * half
+    seg_id = iota((GROUP, seg_dev), 1) + 1
+    for k in reversed(across):
+        await_group(r1, 0, k, asked_rows)
+        asked = strided_group(r1, params, k).astype(I32)
+        chunk, col = asked >> 7, asked & (LANES - 1)
+        picked = [jnp.zeros((GROUP, LANES), F32) for _ in range(params)]
+        for h in range(chunks):
+            here = chunk == h
+            for p in range(params):
+                row = src_v[p : p + 1, h * LANES : (h + 1) * LANES]
+                picked[p] = jnp.where(here, lanes_of(row, col), picked[p])
+        total = jnp.zeros((GROUP, LANES), F32)
+        for p in range(params):
+            total = total + strided_group(r1, p, k) * picked[p]
+        put_group(s2, 0, k, total)
+        segs = strided_group(r1, params + 1, k).astype(I32)
+        pick = jnp.concatenate(
+            [
+                jnp.broadcast_to(segs[:, r : r + 1], (GROUP, seg_dev)) == seg_id
+                for r in range(SLOT_T)
+            ],
+            axis=0,
+        ).astype(F32).astype(BF16)
+        both = jnp.dot(pick, att_pair, preferred_element_type=F32)
+        rows = both[:, :cols] + both[:, cols:]
+        for r in range(SLOT_T):
+            for c in range(half):
+                put_group(
+                    s2, 1 + r * half + c, k,
+                    rows[r * GROUP : (r + 1) * GROUP, c * LANES : (c + 1) * LANES],
+                )
+        send_group(s2, r2, 1, k, 0, answer_rows)
+    keep(s2, r2)
 
     asked = strided(r1, params).astype(I32)
     chunk, col = asked >> 7, asked & (LANES - 1)
-    picked = [jnp.zeros((nb, LANES), F32) for _ in range(params)]
-    for h in range(chunks):
-        here = chunk == h
-        for k in range(params):
-            row = src_v[k : k + 1, h * LANES : (h + 1) * LANES]
-            picked[k] = jnp.where(here, lanes_of(row, col), picked[k])
-    total = jnp.zeros((nb, LANES), F32)
-    for k in range(params):
-        total = total + strided(r1, k) * picked[k]
-    put(s2, 0, total)
-    segs = strided(r1, params + 1).astype(I32)
-    seg_id = iota((nb, seg_dev), 1) + 1
-    att_pair = jnp.concatenate(halves(att_v[...]), axis=1)
-    choice = []
-    for r in range(SLOT_T):
-        pick = jnp.broadcast_to(segs[:, r : r + 1], (nb, seg_dev)) == seg_id
-        choice.append(pick.astype(F32).astype(BF16))
-        both = jnp.dot(choice[r], att_pair, preferred_element_type=F32)
-        rows = both[:, :cols] + both[:, cols:]
-        for c in range(half):
-            put(s2, 1 + r * half + c, rows[:, c * LANES : (c + 1) * LANES])
-    for k in range(1 + SLOT_T * half, ROWS_MSG):
-        put(s2, k, jnp.zeros((nb, LANES), F32))
-    exchange(s2, r2, 1)
-
     for p in range(nb):
         low_v[:, p * LANES : (p + 1) * LANES] = (
             jnp.broadcast_to(col[p : p + 1], (LANES, LANES)) == slot_id
         ).astype(F32).astype(BF16)
-    obs_t, obs_row = iota((td, LANES), 0), iota((td, LANES), 1)
-    count = jnp.zeros((td, LANES), I32)
-    for t in range(td):
-        count = jnp.where(obs_t == t, cnt_ref[t], count)
-    live = obs_row < count
-
-    await_bytes(r2, (n_tm - 1) * ROWS_MSG, recv_sem.at[1])
-
+    segs = strided(r1, params + 1).astype(I32)
+    choice = jnp.concatenate(
+        [
+            jnp.broadcast_to(segs[:, r : r + 1], (nb, seg_dev)) == iota((nb, seg_dev), 1) + 1
+            for r in range(SLOT_T)
+        ],
+        axis=0,
+    ).astype(F32).astype(BF16)
+
+    rank = rank_v[...]
+    source = jnp.zeros((td, LANES), F32)
+    for k in reversed(across):
+        await_group(r2, 1, k, answer_rows)
+        answers = strided_group(r2, 0, k)
+        first = jnp.bitwise_xor(my_group, k) * GROUP
+        for w in range(GROUP):
+            source = jnp.where(owner == first + w, lanes_of(answers[w : w + 1], rank), source)
     for t in range(td):
         for c in range(half):
             dir_v[t : t + 1, c * LANES : (c + 1) * LANES] = r2[
@@ -217,17 +272,11 @@
     part = jnp.zeros((td, LANES), F32)
     for t in range(td):
         part = jnp.where(obs_t == t, sums[:, t * LANES : (t + 1) * LANES], part)
-    answers = strided(r2, 0)
-    rank = rank_v[...]
-    source = jnp.zeros((td, LANES), F32)
-    for b in range(nb):
-        source = jnp.where(owner == b, lanes_of(answers[b : b + 1], rank), source)
     projected = jnp.where(live, part + source, 0.0)
     proj_o[...] = projected
     weighted = wgt_v[...] * projected
     curvature = jnp.sum(projected * weighted)
 
-    put(s3, 0, to_slots(weighted))
     w_hi, w_lo = halves(weighted)
     w_hi, w_lo = w_hi.astype(F32), w_lo.astype(F32)
     slots = iota((SLOT_T * nb, LANES), 0)
@@ -254,44 +303,55 @@
     for r in range(SLOT_T):
         for c in range(half):
             put(
-                s3, 1 + r * half + c,
+                s3, r * half + c,
                 grad[r * nb : (r + 1) * nb, c * LANES : (c + 1) * LANES],
             )
-    put(s3, 1 + SLOT_T * half, jnp.full((nb, LANES), curvature, F32))
-    for k in range(2 + SLOT_T * half, ROWS_MSG):
-        put(s3, k, jnp.zeros((nb, LANES), F32))
-    exchange(s3, r3, 2)
-    await_bytes(r3, (n_tm - 1) * ROWS_MSG, recv_sem.at[2])
-
-    zrows = seg_dev * half + 8
+    curv_row = SLOT_T * half
+    put(s3, curv_row, jnp.full((nb, LANES), curvature, F32))
+    for k in across:
+        send_group(s3, r3, 2, k, 0, curv_row + 1)
+    weight_row = curv_row + 1
+    put(s3, weight_row, to_slots(weighted))
+    for k in across:
+        send_group(s3, r3, 3, k, weight_row, 1)
+    keep(s3, r3)
+    for k in across:
+        await_group(r3, 2, k, curv_row + 1)
+
+    zrows = seg_dev * half + 1
+    pitch = rz.shape[0] // n_sky
 
     def zblock(q):
-        return pl.ds(pl.multiple_of(q * zrows, 8), zrows)
-
-    owned = jnp.zeros((seg_dev, cols), F32)
-    for r in range(SLOT_T):
-        rows = jnp.concatenate([strided(r3, 1 + r * half + c) for c in range(half)], axis=1)
-        both = lax.dot_general(
-            choice[r], jnp.concatenate(halves(rows), axis=1), TN, preferred_element_type=F32
-        )
-        owned = owned + both[:, :cols] + both[:, cols:]
+        return pl.ds(pl.multiple_of(q * pitch, 8), zrows)
+
+    rows = jnp.concatenate(
+        [
+            jnp.concatenate([strided(r3, r * half + c) for c in range(half)], axis=1)
+            for r in range(SLOT_T)
+        ],
+        axis=0,
+    )
+    both = lax.dot_general(
+        choice, jnp.concatenate(halves(rows), axis=1), TN, preferred_element_type=F32
+    )
+    owned = both[:, :cols] + both[:, cols:]
     for c in range(half):
         sz[c * seg_dev : (c + 1) * seg_dev, :] = owned[:, c * LANES : (c + 1) * LANES]
-    curv_rows = jnp.sum(strided(r3, 1 + SLOT_T * half), axis=0, keepdims=True)
-    sz[seg_dev * half : zrows, :] = jnp.broadcast_to(curv_rows, (8, LANES))
-
-    @pl.loop(1, n_sky)
-    def _(i):
+    sz[zrows - 1 : zrows, :] = jnp.sum(strided(r3, curv_row), axis=0, keepdims=True)
+
+    for i in sorted(range(1, n_sky), key=lambda i: -min(i, n_sky - i)):
         q = lax.rem(z + i, n_sky)
         pltpu.make_async_remote_copy(
-            src_ref=sz, dst_ref=rz.at[zblock(z)],
-            send_sem=send_sem.at[3], recv_sem=recv_sem.at[3],
+            src_ref=sz.at[pl.ds(0, zrows)], dst_ref=rz.at[zblock(z)],
+            send_sem=zsend_sem.at[0], recv_sem=zrecv_sem.at[0],
             device_id=(q, me), device_id_type=pl.DeviceIdType.MESH,
         ).start()
 
-    rz[zblock(z), :] = sz[...]
-
-    back = strided(r3, 0)
+    rz[zblock(z), :] = sz[0:zrows, :]
+
+    for k in across:
+        await_group(r3, 3, k, 1)
+    back = strided(r3, weight_row)
     chunk_id = iota((chunks, LANES), 0)
     terms = []
     for k in range(params):
@@ -321,38 +381,47 @@
                 k * chunks + h : k * chunks + h + 1
             ]
 
-    await_bytes(rz, (n_sky - 1) * zrows, recv_sem.at[3])
+    for k, (ref, rows) in enumerate(
+        ((s1, asked_rows), (s2, answer_rows), (s3, curv_row + 1), (s3, 1))
+    ):
+        await_bytes(ref, (n_tm - 1) * rows, send_sem.at[k])
+    await_bytes(rz, (n_sky - 1) * zrows, zrecv_sem.at[0])
     summed = rz[0:zrows, :]
     for q in range(1, n_sky):
-        summed = summed + rz[q * zrows : (q + 1) * zrows, :]
+        summed = summed + rz[q * pitch : q * pitch + zrows, :]
+    sums_o[0:zrows, :] = summed
+    await_bytes(rz, (n_sky - 1) * zrows, zsend_sem.at[0])
+
+
+def hand_over(proj, sums, src, proj_o, att_o, src_o, curv_o):
+    seg_dev, cols = att_o.shape
+    half = cols // LANES
+    proj_o[...] = proj[...]
+    src_o[...] = src[...]
     for c in range(half):
-        att_o[:, c * LANES : (c + 1) * LANES] = summed[c * seg_dev : (c + 1) * seg_dev]
-    curv_o[0] = summed[seg_dev * half, 0]
-
-    for k, ref in enumerate((s1, s2, s3)):
-        await_bytes(ref, (n_tm - 1) * ROWS_MSG, send_sem.at[k])
-    await_bytes(rz, (n_sky - 1) * zrows, send_sem.at[3])
+        att_o[:, c * LANES : (c + 1) * LANES] = sums[c * seg_dev : (c + 1) * seg_dev, :]
+    curv_o[0] = sums[seg_dev * half, 0]
 
 
 def per_device(n_sky, n_tm, tiles, tile_seg, tile_count, src_index, src_coef, obs_weight, att_dir, src_dir):
     td, rows, cols = tiles.shape
     params, src_dev = src_dir.shape
     seg_dev = att_dir.shape[0]
+    groups = n_tm // GROUP
     msg = pltpu.VMEM((n_tm * ROWS_MSG, LANES), F32)
-    zrows = seg_dev * (cols // LANES) + 8
+    pitch = seg_dev * (cols // LANES) + 8
     vmem, smem, hbm = (
         pl.BlockSpec(memory_space=s) for s in (pltpu.VMEM, pltpu.SMEM, pl.ANY)
     )
-    projected, att_normal, src_normal, curvature = pl.pallas_call(
+    projected, sums, src_normal = pl.pallas_call(
         functools.partial(kernel, n_sky, n_tm),
         out_shape=(
             jax.ShapeDtypeStruct((td, rows), F32),
-            jax.ShapeDtypeStruct((seg_dev, cols), F32),
+            jax.ShapeDtypeStruct((pitch, LANES), F32),
             jax.ShapeDtypeStruct((params, src_dev), F32),
-            jax.ShapeDtypeStruct((1,), F32),
         ),
         in_specs=[smem, smem, hbm, hbm, hbm, hbm, hbm, hbm],
-        out_specs=(vmem, vmem, vmem, smem),
+        out_specs=(vmem, vmem, vmem),
         scratch_shapes=[
             pltpu.VMEM((td, rows, cols), F32),
             pltpu.VMEM((td, rows), I32),
@@ -367,16 +436,30 @@
             pltpu.VMEM((td, rows), I32),
             pltpu.VMEM((2 * n_tm, LANES), I32),
             msg, msg, msg, msg, msg, msg,
-            pltpu.VMEM((zrows, LANES), F32),
-            pltpu.VMEM((n_sky * zrows, LANES), F32),
+            pltpu.VMEM((pitch, LANES), F32),
+            pltpu.VMEM((n_sky * pitch, LANES), F32),
             pltpu.SemaphoreType.DMA((6,)),
             pltpu.SemaphoreType.DMA((4,)),
-            pltpu.SemaphoreType.DMA((4,)),
+            pltpu.SemaphoreType.DMA((4, groups)),
+            pltpu.SemaphoreType.DMA((1,)),
+            pltpu.SemaphoreType.DMA((1,)),
         ],
         compiler_params=pltpu.CompilerParams(
-            collective_id=0, has_side_effects=True, vmem_limit_bytes=48 << 20
+            collective_id=0, has_side_effects=True, vmem_limit_bytes=SCOPED
         ),
     )(tile_seg, tile_count, tiles, src_index, src_coef, obs_weight, att_dir, src_dir)
+    projected, att_normal, src_normal, curvature = pl.pallas_call(
+        hand_over,
+        out_shape=(
+            jax.ShapeDtypeStruct((td, rows), F32),
+            jax.ShapeDtypeStruct((seg_dev, cols), F32),
+            jax.ShapeDtypeStruct((params, src_dev), F32),
+            jax.ShapeDtypeStruct((1,), F32),
+        ),
+        in_specs=[vmem, vmem, vmem],
+        out_specs=(vmem, vmem, vmem, smem),
+        compiler_params=pltpu.CompilerParams(vmem_limit_bytes=SCOPED),
+    )(projected, sums, src_normal)
     return projected, att_normal, src_normal, curvature.reshape(())
 
 

time: 48 us -> 35.5 us (0.74)
  local copies, waits for them, and re-layouts: 8.55 us -> 0 us
  between operations: 2.47 us -> 0.64 us
  Pallas kernels: 36.6 us -> 34.8 us
    unnamed x19 -> x0, local copies, waits for them, and re-layouts: 8.55 us -> none
    pallas_call x1, Pallas kernels: 36.6 us -> 33.1 us  [per_device(): pl.pallas_call(functools.partial(kernel, n_sky, n_tm), out_shape=(jax.Sha...]
    pallas_call x0 -> x1, Pallas kernels: none -> 1.62 us  [per_device(): pl.pallas_call(hand_over, out_shape=(jax.ShapeDtypeStruct((td, rows), F32...]
where the time goes in v2:
time: 35.5 us; the launch traced here: 35.4 us
  Pallas kernels  34.8 us (98%)
  between operations  0.64 us (2%)
    pallas_call x1, Pallas kernels, per_device(): pl.pallas_call(functools.partial(kernel, n_sky, n_tm), out_shape=(jax.Sha...  33.1 us
    pallas_call x1, Pallas kernels, per_device(): pl.pallas_call(hand_over, out_shape=(jax.ShapeDtypeStruct((td, rows), F32...  1.62 us

profile of v2, /device:TPU:1, one launch (start us, length us, event | category | flops | bytes accessed | tf_op | source)
XLA Modules:
  0.0 35.4 jit_solution(13503126271564702961)
XLA Ops:
  0.6 33.1 %shard_map.111 = (f32[16,128]{1,0:T(8,128)}, f32[40,128]{1,0:T(8,128)}, f32[5,4096]{1,0:T(8,128)}) custom-call(s32[16]{0:T(128)} %seg_ref.1, s32[16]{0:T(128)} %cnt_ref.1, f32[16,128,256]{2,1,0:T(8,128)} %tiles_hbm.1, s32[16,128]{1,0:T(8,128)} %idx_hbm.1, f32[5,16,128]{2,1,0:T(8,128)} %coef_hbm.1, f32[16,128]{1,0:T(8,128)} %wgt_hbm.1, f32[16,256]{1,0:T(8,128)} %att_hbm.1, ...), custom_call_target="tpu_custom_call" | custom-call | tf_op jit(solution)/shard_map/pallas_call | solution.py:416
  33.8 1.6 %shard_map.112 = (f32[16,128]{1,0:T(8,128)}, f32[16,256]{1,0:T(8,128)}, f32[5,4096]{1,0:T(8,128)}, f32[1]{0:T(128)}) custom-call(f32[16,128]{1,0:T(8,128)} %get-tuple-element.11.proj, f32[40,128]{1,0:T(8,128)} %get-tuple-element.12.sums, f32[5,4096]{1,0:T(8,128)} %get-tuple-element.13.src), custom_call_target="tpu_custom_call" | custom-call | tf_op jit(solution)/shard_map/pallas_call | solution.py:451

commit v3 on v2

--- a/solution.py
+++ b/solution.py
@@ -10,11 +10,10 @@
 LANES = 128
 ROWS_MSG = 8
 GROUP = 8
-SCOPED = 58 << 20
+SCOPED = 44 << 20
 SLOT_T = 2
 F32, BF16, I32 = jnp.float32, jnp.bfloat16, jnp.int32
 NT = (((1,), (1,)), ((), ()))
-TN = (((0,), (0,)), ((), ()))
 
 
 def halves(x):
@@ -41,9 +40,9 @@
 
 def kernel(
     n_sky, n_tm,
-    seg_ref, cnt_ref, tiles_hbm, idx_hbm, coef_hbm, wgt_hbm, att_hbm, src_hbm,
+    seg_hbm, cnt_hbm, tiles_hbm, idx_hbm, coef_hbm, wgt_hbm, att_hbm, src_hbm,
     proj_o, sums_o, src_o,
-    tiles_v, idx_v, coef_v, wgt_v, att_v, src_v, thi, tlo, low_v, dir_v, rank_v, inv_v,
+    seg_ref, cnt_ref, tiles_v, idx_v, coef_v, wgt_v, att_v, src_v, thi, tlo, thi_t, tlo_t, low_v, dir_v, rank_v, inv_v,
     s1, r1, s2, r2, s3, r3, sz, rz,
     in_sem, send_sem, recv_sem, zsend_sem, zrecv_sem,
 ):
@@ -59,25 +58,27 @@
     across = sorted(range(groups), key=lambda k: -min(k, groups - k))
     within = sorted(range(GROUP), key=lambda k: -hops(k, (4, 2)))
 
+    barrier = pltpu.get_barrier_semaphore()
+
+    for k in across:
+        for j in within:
+            if k or j:
+                q = jnp.bitwise_xor(me, k * GROUP + j)
+                pl.semaphore_signal(barrier, 1, device_id=(z, q))
+
+    @pl.loop(1, n_sky)
+    def _(i):
+        pl.semaphore_signal(barrier, 1, device_id=(lax.rem(z + i, n_sky), me))
+
     loads = [
         pltpu.make_async_copy(a, b, in_sem.at[i])
         for i, (a, b) in enumerate(
             ((idx_hbm, idx_v), (coef_hbm, coef_v), (src_hbm, src_v), (att_hbm, att_v),
-             (wgt_hbm, wgt_v), (tiles_hbm, tiles_v))
+             (wgt_hbm, wgt_v), (tiles_hbm, tiles_v), (seg_hbm, seg_ref), (cnt_hbm, cnt_ref))
         )
     ]
     for copy in loads:
         copy.start()
-
-    barrier = pltpu.get_barrier_semaphore()
-
-    @pl.loop(1, n_tm)
-    def _(i):
-        pl.semaphore_signal(barrier, 1, device_id=(z, jnp.bitwise_xor(me, i)))
-
-    @pl.loop(1, n_sky)
-    def _(i):
-        pl.semaphore_signal(barrier, 1, device_id=(lax.rem(z + i, n_sky), me))
 
     def strided(ref, row):
         return ref[pl.ds(row, nb, stride=ROWS_MSG), :]
@@ -119,22 +120,7 @@
     def await_group(ref, phase, k, rows):
         await_bytes(ref, (GROUP - (k == 0)) * rows, recv_sem.at[phase, k])
 
-    seg_shift = seg_dev.bit_length() - 1
-    owner_t = [seg_ref[t] >> seg_shift for t in range(td)]
-    local_t = [seg_ref[t] & (seg_dev - 1) for t in range(td)]
-    rank_t = []
-    for t in range(td):
-        r = jnp.int32(0)
-        for before in range(t):
-            r = r + (owner_t[before] == owner_t[t]).astype(I32)
-        rank_t.append(r)
     bins, lane = iota((nb, LANES), 0), iota((nb, LANES), 1)
-    wanted = jnp.zeros((nb, LANES), I32)
-    for t in range(td):
-        hit = (bins == owner_t[t]) & (lane == rank_t[t])
-        wanted = jnp.where(hit, local_t[t] + 1, wanted)
-    put(s1, params + 1, wanted.astype(F32))
-
     loads[0].wait()
     src_shift = src_dev.bit_length() - 1
     idx = idx_v[...]
@@ -176,6 +162,22 @@
         put(s1, k, to_slots(coef_v[k]))
     put(s1, params, to_slots((idx & (src_dev - 1)).astype(F32)))
 
+    loads[6].wait()
+    seg_shift = seg_dev.bit_length() - 1
+    owner_t = [seg_ref[t] >> seg_shift for t in range(td)]
+    local_t = [seg_ref[t] & (seg_dev - 1) for t in range(td)]
+    rank_t = []
+    for t in range(td):
+        r = jnp.int32(0)
+        for before in range(t):
+            r = r + (owner_t[before] == owner_t[t]).astype(I32)
+        rank_t.append(r)
+    wanted = jnp.zeros((nb, LANES), I32)
+    for t in range(td):
+        hit = (bins == owner_t[t]) & (lane == rank_t[t])
+        wanted = jnp.where(hit, local_t[t] + 1, wanted)
+    put(s1, params + 1, wanted.astype(F32))
+
     asked_rows = params + 2
     pl.semaphore_wait(barrier, n_tm + n_sky - 2)
     for k in across:
@@ -190,8 +192,11 @@
         hi, lo = halves(tiles_v[t])
         thi[rows, :] = hi
         tlo[rows, :] = lo
-
-    for copy in (loads[2], loads[3], loads[4]):
+        hi, lo = halves(tiles_v[t].T)
+        thi_t[:, rows] = hi
+        tlo_t[:, rows] = lo
+
+    for copy in (loads[2], loads[3], loads[4], loads[7]):
         copy.wait()
     att_pair = jnp.concatenate(halves(att_v[...]), axis=1)
     obs_t, obs_row = iota((td, LANES), 0), iota((td, LANES), 1)
@@ -244,11 +249,12 @@
     segs = strided(r1, params + 1).astype(I32)
     choice = jnp.concatenate(
         [
-            jnp.broadcast_to(segs[:, r : r + 1], (nb, seg_dev)) == iota((nb, seg_dev), 1) + 1
+            jnp.broadcast_to(segs[:, r : r + 1], (nb, LANES)) == iota((nb, LANES), 1) + 1
             for r in range(SLOT_T)
         ],
         axis=0,
-    ).astype(F32).astype(BF16)
+    ).astype(F32)
+    choice = choice.T[:seg_dev].astype(BF16)
 
     rank = rank_v[...]
     source = jnp.zeros((td, LANES), F32)
@@ -264,10 +270,10 @@
                 pl.ds(owner_t[t] * ROWS_MSG + 1 + rank_t[t] * half + c, 1), :
             ]
     dir_hi, dir_lo = halves(dir_v[...])
-    first = lax.dot_general(
-        jnp.concatenate([dir_hi, dir_lo], axis=0), thi[...], NT, preferred_element_type=F32
-    )
-    second = lax.dot_general(dir_hi, tlo[...], NT, preferred_element_type=F32)
+    first = jnp.dot(
+        jnp.concatenate([dir_hi, dir_lo], axis=0), thi_t[...], preferred_element_type=F32
+    )
+    second = jnp.dot(dir_hi, tlo_t[...], preferred_element_type=F32)
     sums = first[:td] + first[td:] + second
     part = jnp.zeros((td, LANES), F32)
     for t in range(td):
@@ -275,7 +281,7 @@
     projected = jnp.where(live, part + source, 0.0)
     proj_o[...] = projected
     weighted = wgt_v[...] * projected
-    curvature = jnp.sum(projected * weighted)
+    curvature = jnp.sum(projected * weighted, axis=0, keepdims=True)
 
     w_hi, w_lo = halves(weighted)
     w_hi, w_lo = w_hi.astype(F32), w_lo.astype(F32)
@@ -307,7 +313,7 @@
                 grad[r * nb : (r + 1) * nb, c * LANES : (c + 1) * LANES],
             )
     curv_row = SLOT_T * half
-    put(s3, curv_row, jnp.full((nb, LANES), curvature, F32))
+    put(s3, curv_row, jnp.broadcast_to(curvature, (nb, LANES)))
     for k in across:
         send_group(s3, r3, 2, k, 0, curv_row + 1)
     weight_row = curv_row + 1
@@ -331,8 +337,8 @@
         ],
         axis=0,
     )
-    both = lax.dot_general(
-        choice, jnp.concatenate(halves(rows), axis=1), TN, preferred_element_type=F32
+    both = jnp.dot(
+        choice, jnp.concatenate(halves(rows), axis=1), preferred_element_type=F32
     )
     owned = both[:, :cols] + both[:, cols:]
     for c in range(half):
@@ -400,7 +406,7 @@
     src_o[...] = src[...]
     for c in range(half):
         att_o[:, c * LANES : (c + 1) * LANES] = sums[c * seg_dev : (c + 1) * seg_dev, :]
-    curv_o[0] = sums[seg_dev * half, 0]
+    curv_o[0] = jnp.sum(sums[seg_dev * half : seg_dev * half + 1, :])
 
 
 def per_device(n_sky, n_tm, tiles, tile_seg, tile_count, src_index, src_coef, obs_weight, att_dir, src_dir):
@@ -420,9 +426,11 @@
             jax.ShapeDtypeStruct((pitch, LANES), F32),
             jax.ShapeDtypeStruct((params, src_dev), F32),
         ),
-        in_specs=[smem, smem, hbm, hbm, hbm, hbm, hbm, hbm],
+        in_specs=[hbm, hbm, hbm, hbm, hbm, hbm, hbm, hbm],
         out_specs=(vmem, vmem, vmem),
         scratch_shapes=[
+            pltpu.SMEM((td,), I32),
+            pltpu.SMEM((td,), I32),
             pltpu.VMEM((td, rows, cols), F32),
             pltpu.VMEM((td, rows), I32),
             pltpu.VMEM((params, td, rows), F32),
@@ -431,6 +439,8 @@
             pltpu.VMEM((params, src_dev), F32),
             pltpu.VMEM((td * rows, cols), BF16),
             pltpu.VMEM((td * rows, cols), BF16),
+            pltpu.VMEM((cols, td * rows), BF16),
+            pltpu.VMEM((cols, td * rows), BF16),
             pltpu.VMEM((LANES, n_tm * LANES), BF16),
             pltpu.VMEM((td, cols), F32),
             pltpu.VMEM((td, rows), I32),
@@ -438,7 +448,7 @@
             msg, msg, msg, msg, msg, msg,
             pltpu.VMEM((pitch, LANES), F32),
             pltpu.VMEM((n_sky * pitch, LANES), F32),
-            pltpu.SemaphoreType.DMA((6,)),
+            pltpu.SemaphoreType.DMA((8,)),
             pltpu.SemaphoreType.DMA((4,)),
             pltpu.SemaphoreType.DMA((4, groups)),
             pltpu.SemaphoreType.DMA((1,)),
@@ -447,7 +457,14 @@
         compiler_params=pltpu.CompilerParams(
             collective_id=0, has_side_effects=True, vmem_limit_bytes=SCOPED
         ),
-    )(tile_seg, tile_count, tiles, src_index, src_coef, obs_weight, att_dir, src_dir)
+    )(
+        *[
+            pltpu.with_memory_space_constraint(x, pltpu.HBM)
+            for x in (
+                tile_seg, tile_count, tiles, src_index, src_coef, obs_weight, att_dir, src_dir,
+            )
+        ]
+    )
     projected, att_normal, src_normal, curvature = pl.pallas_call(
         hand_over,
         out_shape=(

time: 35.5 us -> 32.9 us (0.927)
  Pallas kernels: 34.8 us -> 32.2 us
    pallas_call x1, Pallas kernels: 33.1 us -> 31.5 us  [per_device(): pl.pallas_call(functools.partial(kernel, n_sky, n_tm), out_shape=(jax.Sha...]
    pallas_call x1, Pallas kernels: 1.62 us -> 0.68 us  [per_device(): pl.pallas_call(hand_over, out_shape=(jax.ShapeDtypeStruct((td, rows), F32...]
where the time goes in v3:
time: 32.9 us; the launch traced here: 32.8 us
  Pallas kernels  32.2 us (98%)
  between operations  0.64 us (2%)
    pallas_call x1, Pallas kernels, per_device(): pl.pallas_call(functools.partial(kernel, n_sky, n_tm), out_shape=(jax.Sha...  31.5 us
    pallas_call x1, Pallas kernels, per_device(): pl.pallas_call(hand_over, out_shape=(jax.ShapeDtypeStruct((td, rows), F32...  0.68 us

profile of v3, /device:TPU:1, one launch (start us, length us, event | category | flops | bytes accessed | tf_op | source)
XLA Modules:
  0.0 32.8 jit_solution(8190655754849468583)
XLA Ops:
  0.6 31.5 %shard_map.111 = (f32[16,128]{1,0:T(8,128)S(1)}, f32[40,128]{1,0:T(8,128)S(1)}, f32[5,4096]{1,0:T(8,128)S(1)}) custom-call(s32[16]{0:T(128)} %seg_hbm.1, s32[16]{0:T(128)} %cnt_hbm.1, f32[16,128,256]{2,1,0:T(8,128)} %tiles_hbm.1, s32[16,128]{1,0:T(8,128)} %idx_hbm.1, f32[5,16,128]{2,1,0:T(8,128)} %coef_hbm.1, f32[16,128]{1,0:T(8,128)} %wgt_hbm.1, ...), custom_call_target="tpu_custom_call" | custom-call | tf_op jit(solution)/shard_map/pallas_call | solution.py:422
  32.1 0.7 %shard_map.112 = (f32[16,128]{1,0:T(8,128)}, f32[16,256]{1,0:T(8,128)}, f32[5,4096]{1,0:T(8,128)}, f32[1]{0:T(128)}) custom-call(f32[16,128]{1,0:T(8,128)S(1)} %get-tuple-element.11.proj, f32[40,128]{1,0:T(8,128)S(1)} %get-tuple-element.12.sums, f32[5,4096]{1,0:T(8,128)S(1)} %get-tuple-element.13.src), custom_call_target="tpu_custom_call" | custom-call | tf_op jit(solution)/shard_map/pallas_call | solution.py:468

commit v4 on v3

--- a/solution.py
+++ b/solution.py
@@ -10,6 +10,7 @@
 LANES = 128
 ROWS_MSG = 8
 GROUP = 8
+PACKED = 16
 SCOPED = 44 << 20
 SLOT_T = 2
 F32, BF16, I32 = jnp.float32, jnp.bfloat16, jnp.int32
@@ -42,7 +43,7 @@
     n_sky, n_tm,
     seg_hbm, cnt_hbm, tiles_hbm, idx_hbm, coef_hbm, wgt_hbm, att_hbm, src_hbm,
     proj_o, sums_o, src_o,
-    seg_ref, cnt_ref, tiles_v, idx_v, coef_v, wgt_v, att_v, src_v, thi, tlo, thi_t, tlo_t, low_v, dir_v, rank_v, inv_v,
+    seg_ref, cnt_ref, tiles_v, idx_v, coef_v, wgt_v, att_v, src_v, thi, tlo, thi_t, tlo_t, slot_v, low_v, dir_v, rank_v, inv_v,
     s1, r1, s2, r2, s3, r3, sz, rz,
     in_sem, send_sem, recv_sem, zsend_sem, zrecv_sem,
 ):
@@ -184,6 +185,12 @@
         send_group(s1, r1, 0, k, 0, asked_rows)
     keep(s1, r1)
 
+    n_slots = SLOT_T * nb
+    slots = iota((n_slots, LANES), 0)
+    for t in range(td):
+        slot_v[:, t * LANES : (t + 1) * LANES] = (
+            (slots == rank_t[t] * nb + owner_t[t]).astype(F32).astype(BF16)
+        )
     loads[5].wait()
 
     @pl.loop(0, td)
@@ -198,7 +205,6 @@
 
     for copy in (loads[2], loads[3], loads[4], loads[7]):
         copy.wait()
-    att_pair = jnp.concatenate(halves(att_v[...]), axis=1)
     obs_t, obs_row = iota((td, LANES), 0), iota((td, LANES), 1)
     count = jnp.zeros((td, LANES), I32)
     for t in range(td):
@@ -206,9 +212,18 @@
     live = obs_row < count
 
     answer_rows = 1 + SLOT_T * half
-    seg_id = iota((GROUP, seg_dev), 1) + 1
-    for k in reversed(across):
-        await_group(r1, 0, k, asked_rows)
+    @pl.loop(0, groups)
+    def _(i):
+        k = jnp.bitwise_xor(i, i >> 1)
+
+        @pl.when(i == 0)
+        def _():
+            await_group(r1, 0, 0, asked_rows)
+
+        @pl.when(i > 0)
+        def _():
+            await_bytes(r1, GROUP * asked_rows, recv_sem.at[0, k])
+
         asked = strided_group(r1, params, k).astype(I32)
         chunk, col = asked >> 7, asked & (LANES - 1)
         picked = [jnp.zeros((GROUP, LANES), F32) for _ in range(params)]
@@ -222,22 +237,28 @@
             total = total + strided_group(r1, p, k) * picked[p]
         put_group(s2, 0, k, total)
         segs = strided_group(r1, params + 1, k).astype(I32)
-        pick = jnp.concatenate(
-            [
-                jnp.broadcast_to(segs[:, r : r + 1], (GROUP, seg_dev)) == seg_id
-                for r in range(SLOT_T)
-            ],
-            axis=0,
-        ).astype(F32).astype(BF16)
-        both = jnp.dot(pick, att_pair, preferred_element_type=F32)
-        rows = both[:, :cols] + both[:, cols:]
         for r in range(SLOT_T):
+            seg = jnp.broadcast_to(segs[:, r : r + 1], (GROUP, LANES))
+            rows = [jnp.zeros((GROUP, LANES), F32) for _ in range(half)]
+            for n in range(seg_dev):
+                here = seg == n + 1
+                for c in range(half):
+                    row = att_v[n : n + 1, c * LANES : (c + 1) * LANES]
+                    rows[c] = jnp.where(here, jnp.broadcast_to(row, here.shape), rows[c])
             for c in range(half):
-                put_group(
-                    s2, 1 + r * half + c, k,
-                    rows[r * GROUP : (r + 1) * GROUP, c * LANES : (c + 1) * LANES],
-                )
-        send_group(s2, r2, 1, k, 0, answer_rows)
+                put_group(s2, 1 + r * half + c, k, rows[c])
+        for j in within:
+
+            @pl.when((i > 0) | (j > 0))
+            def _(j=j):
+                q = jnp.bitwise_xor(me, k * GROUP + j)
+                pltpu.make_async_remote_copy(
+                    src_ref=s2.at[block(q, 0, answer_rows)],
+                    dst_ref=r2.at[block(me, 0, answer_rows)],
+                    send_sem=send_sem.at[1], recv_sem=recv_sem.at[1, k],
+                    device_id=(z, q), device_id_type=pl.DeviceIdType.MESH,
+                ).start()
+
     keep(s2, r2)
 
     asked = strided(r1, params).astype(I32)
@@ -283,23 +304,15 @@
     weighted = wgt_v[...] * projected
     curvature = jnp.sum(projected * weighted, axis=0, keepdims=True)
 
-    w_hi, w_lo = halves(weighted)
-    w_hi, w_lo = w_hi.astype(F32), w_lo.astype(F32)
-    slots = iota((SLOT_T * nb, LANES), 0)
     left = []
-    for t in range(td):
-        here = slots == rank_t[t] * nb + owner_t[t]
-        left.append(
-            jnp.concatenate(
-                [
-                    jnp.where(here, jnp.broadcast_to(w[t : t + 1], slots.shape), 0.0)
-                    for w in (w_hi, w_lo)
-                ],
-                axis=0,
-            ).astype(BF16)
-        )
-    left = jnp.concatenate(left, axis=1)
-    n_slots = SLOT_T * nb
+    for w in halves(weighted):
+        w = w.astype(F32)
+        spread = [
+            jnp.broadcast_to(w[t : t + 1], (PACKED, LANES)).astype(BF16) for t in range(td)
+        ]
+        row = jnp.concatenate(spread, axis=1)
+        left.append(jnp.concatenate([row] * (n_slots // PACKED), axis=0) * slot_v[...])
+    left = jnp.concatenate(left, axis=0)
     grad = jnp.dot(left, thi[...], preferred_element_type=F32)
     grad = (
         grad[:n_slots]
@@ -441,6 +454,7 @@
             pltpu.VMEM((td * rows, cols), BF16),
             pltpu.VMEM((cols, td * rows), BF16),
             pltpu.VMEM((cols, td * rows), BF16),
+            pltpu.VMEM((SLOT_T * n_tm, td * rows), BF16),
             pltpu.VMEM((LANES, n_tm * LANES), BF16),
             pltpu.VMEM((td, cols), F32),
             pltpu.VMEM((td, rows), I32),

time: 32.9 us -> 32.7 us (level)
  no operation moved by 1% of the time
where the time goes in v4:
time: 32.7 us; the launch traced here: 32.6 us
  Pallas kernels  31.9 us (98%)
  between operations  0.64 us (2%)
    pallas_call x1, Pallas kernels, per_device(): pl.pallas_call(functools.partial(kernel, n_sky, n_tm), out_shape=(jax.Sha...  31.3 us
    pallas_call x1, Pallas kernels, per_device(): pl.pallas_call(hand_over, out_shape=(jax.ShapeDtypeStruct((td, rows), F32...  0.68 us

profile of v4, /device:TPU:1, one launch (start us, length us, event | category | flops | bytes accessed | tf_op | source)
XLA Modules:
  0.0 32.6 jit_solution(18249189738993358794)
XLA Ops:
  0.6 31.3 %shard_map.111 = (f32[16,128]{1,0:T(8,128)S(1)}, f32[40,128]{1,0:T(8,128)S(1)}, f32[5,4096]{1,0:T(8,128)S(1)}) custom-call(s32[16]{0:T(128)} %seg_hbm.1, s32[16]{0:T(128)} %cnt_hbm.1, f32[16,128,256]{2,1,0:T(8,128)} %tiles_hbm.1, s32[16,128]{1,0:T(8,128)} %idx_hbm.1, f32[5,16,128]{2,1,0:T(8,128)} %coef_hbm.1, f32[16,128]{1,0:T(8,128)} %wgt_hbm.1, ...), custom_call_target="tpu_custom_call" | custom-call | tf_op jit(solution)/shard_map/pallas_call | solution.py:435
  31.9 0.7 %shard_map.112 = (f32[16,128]{1,0:T(8,128)}, f32[16,256]{1,0:T(8,128)}, f32[5,4096]{1,0:T(8,128)}, f32[1]{0:T(128)}) custom-call(f32[16,128]{1,0:T(8,128)S(1)} %get-tuple-element.11.proj, f32[40,128]{1,0:T(8,128)S(1)} %get-tuple-element.12.sums, f32[5,4096]{1,0:T(8,128)S(1)} %get-tuple-element.13.src), custom_call_target="tpu_custom_call" | custom-call | tf_op jit(solution)/shard_map/pallas_call | solution.py:482

commit v5 on v4

--- a/solution.py
+++ b/solution.py
@@ -121,11 +121,17 @@
     def await_group(ref, phase, k, rows):
         await_bytes(ref, (GROUP - (k == 0)) * rows, recv_sem.at[phase, k])
 
+    loads[7].wait()
+    obs_t, obs_row = iota((td, LANES), 0), iota((td, LANES), 1)
+    count = jnp.zeros((td, LANES), I32)
+    for t in range(td):
+        count = jnp.where(obs_t == t, cnt_ref[t], count)
+    live = obs_row < count
     bins, lane = iota((nb, LANES), 0), iota((nb, LANES), 1)
     loads[0].wait()
     src_shift = src_dev.bit_length() - 1
     idx = idx_v[...]
-    owner = idx >> src_shift
+    owner = jnp.where(live, idx >> src_shift, -1)
     mine = [jnp.broadcast_to(owner[t : t + 1], (nb, LANES)) == bins for t in range(td)]
     ones = [m.astype(F32) for m in mine]
     i0, i1 = iota((LANES, 2 * LANES), 0), iota((LANES, 2 * LANES), 1)
@@ -203,13 +209,8 @@
         thi_t[:, rows] = hi
         tlo_t[:, rows] = lo
 
-    for copy in (loads[2], loads[3], loads[4], loads[7]):
+    for copy in (loads[2], loads[3], loads[4]):
         copy.wait()
-    obs_t, obs_row = iota((td, LANES), 0), iota((td, LANES), 1)
-    count = jnp.zeros((td, LANES), I32)
-    for t in range(td):
-        count = jnp.where(obs_t == t, cnt_ref[t], count)
-    live = obs_row < count
 
     answer_rows = 1 + SLOT_T * half
     @pl.loop(0, groups)

time: 32.7 us -> 32.8 us (level)
  no operation moved by 1% of the time
where the time goes in v5:
time: 32.8 us; the launch traced here: 32.7 us
  Pallas kernels  32.1 us (98%)
  between operations  0.64 us (2%)
    pallas_call x1, Pallas kernels, per_device(): pl.pallas_call(functools.partial(kernel, n_sky, n_tm), out_shape=(jax.Sha...  31.4 us
    pallas_call x1, Pallas kernels, per_device(): pl.pallas_call(hand_over, out_shape=(jax.ShapeDtypeStruct((td, rows), F32...  0.68 us

profile of v5, /device:TPU:1, one launch (start us, length us, event | category | flops | bytes accessed | tf_op | source)
XLA Modules:
  0.0 32.7 jit_solution(5961407941022028222)
XLA Ops:
  0.6 31.4 %shard_map.111 = (f32[16,128]{1,0:T(8,128)S(1)}, f32[40,128]{1,0:T(8,128)S(1)}, f32[5,4096]{1,0:T(8,128)S(1)}) custom-call(s32[16]{0:T(128)} %seg_hbm.1, s32[16]{0:T(128)} %cnt_hbm.1, f32[16,128,256]{2,1,0:T(8,128)} %tiles_hbm.1, s32[16,128]{1,0:T(8,128)} %idx_hbm.1, f32[5,16,128]{2,1,0:T(8,128)} %coef_hbm.1, f32[16,128]{1,0:T(8,128)} %wgt_hbm.1, ...), custom_call_target="tpu_custom_call" | custom-call | tf_op jit(solution)/shard_map/pallas_call | solution.py:436
  32.0 0.7 %shard_map.112 = (f32[16,128]{1,0:T(8,128)}, f32[16,256]{1,0:T(8,128)}, f32[5,4096]{1,0:T(8,128)}, f32[1]{0:T(128)}) custom-call(f32[16,128]{1,0:T(8,128)S(1)} %get-tuple-element.11.proj, f32[40,128]{1,0:T(8,128)S(1)} %get-tuple-element.12.sums, f32[5,4096]{1,0:T(8,128)S(1)} %get-tuple-element.13.src), custom_call_target="tpu_custom_call" | custom-call | tf_op jit(solution)/shard_map/pallas_call | solution.py:483

commit v6 on v5

--- a/solution.py
+++ b/solution.py
@@ -78,8 +78,8 @@
              (wgt_hbm, wgt_v), (tiles_hbm, tiles_v), (seg_hbm, seg_ref), (cnt_hbm, cnt_ref))
         )
     ]
-    for copy in loads:
-        copy.start()
+    for i in (7, 0, 6, 1, 2, 3, 4, 5):
+        loads[i].start()
 
     def strided(ref, row):
         return ref[pl.ds(row, nb, stride=ROWS_MSG), :]

time: 32.8 us -> 32.7 us (level)
  no operation moved by 1% of the time
where the time goes in v6:
time: 32.7 us; the launch traced here: 32.6 us
  Pallas kernels  31.9 us (98%)
  between operations  0.64 us (2%)
    pallas_call x1, Pallas kernels, per_device(): pl.pallas_call(functools.partial(kernel, n_sky, n_tm), out_shape=(jax.Sha...  31.3 us
    pallas_call x1, Pallas kernels, per_device(): pl.pallas_call(hand_over, out_shape=(jax.ShapeDtypeStruct((td, rows), F32...  0.68 us

profile of v6, /device:TPU:1, one launch (start us, length us, event | category | flops | bytes accessed | tf_op | source)
XLA Modules:
  0.0 32.6 jit_solution(3969080223398347382)
XLA Ops:
  0.6 31.3 %shard_map.111 = (f32[16,128]{1,0:T(8,128)S(1)}, f32[40,128]{1,0:T(8,128)S(1)}, f32[5,4096]{1,0:T(8,128)S(1)}) custom-call(s32[16]{0:T(128)} %seg_hbm.1, s32[16]{0:T(128)} %cnt_hbm.1, f32[16,128,256]{2,1,0:T(8,128)} %tiles_hbm.1, s32[16,128]{1,0:T(8,128)} %idx_hbm.1, f32[5,16,128]{2,1,0:T(8,128)} %coef_hbm.1, f32[16,128]{1,0:T(8,128)} %wgt_hbm.1, ...), custom_call_target="tpu_custom_call" | custom-call | tf_op jit(solution)/shard_map/pallas_call | solution.py:436
  31.9 0.7 %shard_map.112 = (f32[16,128]{1,0:T(8,128)}, f32[16,256]{1,0:T(8,128)}, f32[5,4096]{1,0:T(8,128)}, f32[1]{0:T(128)}) custom-call(f32[16,128]{1,0:T(8,128)S(1)} %get-tuple-element.11.proj, f32[40,128]{1,0:T(8,128)S(1)} %get-tuple-element.12.sums, f32[5,4096]{1,0:T(8,128)S(1)} %get-tuple-element.13.src), custom_call_target="tpu_custom_call" | custom-call | tf_op jit(solution)/shard_map/pallas_call | solution.py:483

commit v7 on v6

--- a/solution.py
+++ b/solution.py
@@ -61,15 +61,14 @@
 
     barrier = pltpu.get_barrier_semaphore()
 
+    around = sorted(range(1, n_sky), key=lambda i: -min(i, n_sky - i))
+    for i in around:
+        pl.semaphore_signal(barrier, 1, device_id=(lax.rem(z + i, n_sky), me))
     for k in across:
         for j in within:
             if k or j:
                 q = jnp.bitwise_xor(me, k * GROUP + j)
                 pl.semaphore_signal(barrier, 1, device_id=(z, q))
-
-    @pl.loop(1, n_sky)
-    def _(i):
-        pl.semaphore_signal(barrier, 1, device_id=(lax.rem(z + i, n_sky), me))
 
     loads = [
         pltpu.make_async_copy(a, b, in_sem.at[i])
@@ -99,15 +98,18 @@
     def block(q, first, rows):
         return pl.ds(pl.multiple_of(q * ROWS_MSG, ROWS_MSG) + first, rows)
 
-    def send_group(src, dst, phase, k, first, rows):
-        for j in within:
-            step = k * GROUP + j
-            if step == 0:
-                continue
+    ring = lambda n, extent: min(n, extent - n)
+    others = sorted(
+        range(1, n_tm),
+        key=lambda i: -(ring(i // GROUP, groups) + ring(i % GROUP // 2, GROUP // 2)),
+    )
+
+    def send_all(src, dst, phase, first, rows):
+        for step in others:
             q = jnp.bitwise_xor(me, step)
             pltpu.make_async_remote_copy(
                 src_ref=src.at[block(q, first, rows)], dst_ref=dst.at[block(me, first, rows)],
-                send_sem=send_sem.at[phase], recv_sem=recv_sem.at[phase, k],
+                send_sem=send_sem.at[phase], recv_sem=recv_sem.at[phase, step // GROUP],
                 device_id=(z, q), device_id_type=pl.DeviceIdType.MESH,
             ).start()
 
@@ -187,8 +189,7 @@
 
     asked_rows = params + 2
     pl.semaphore_wait(barrier, n_tm + n_sky - 2)
-    for k in across:
-        send_group(s1, r1, 0, k, 0, asked_rows)
+    send_all(s1, r1, 0, 0, asked_rows)
     keep(s1, r1)
 
     n_slots = SLOT_T * nb
@@ -328,12 +329,10 @@
             )
     curv_row = SLOT_T * half
     put(s3, curv_row, jnp.broadcast_to(curvature, (nb, LANES)))
-    for k in across:
-        send_group(s3, r3, 2, k, 0, curv_row + 1)
+    send_all(s3, r3, 2, 0, curv_row + 1)
     weight_row = curv_row + 1
     put(s3, weight_row, to_slots(weighted))
-    for k in across:
-        send_group(s3, r3, 3, k, weight_row, 1)
+    send_all(s3, r3, 3, weight_row, 1)
     keep(s3, r3)
     for k in across:
         await_group(r3, 2, k, curv_row + 1)
@@ -359,7 +358,7 @@
         sz[c * seg_dev : (c + 1) * seg_dev, :] = owned[:, c * LANES : (c + 1) * LANES]
     sz[zrows - 1 : zrows, :] = jnp.sum(strided(r3, curv_row), axis=0, keepdims=True)
 
-    for i in sorted(range(1, n_sky), key=lambda i: -min(i, n_sky - i)):
+    for i in around:
         q = lax.rem(z + i, n_sky)
         pltpu.make_async_remote_copy(
             src_ref=sz.at[pl.ds(0, zrows)], dst_ref=rz.at[zblock(z)],

time: 32.7 us -> 32.3 us (0.988)
    pallas_call x1, Pallas kernels: 31.3 us -> 30.9 us  [per_device(): pl.pallas_call(functools.partial(kernel, n_sky, n_tm), out_shape=(jax.Sha...]
where the time goes in v7:
time: 32.3 us; the launch traced here: 32.2 us
  Pallas kernels  31.6 us (98%)
  between operations  0.64 us (2%)
    pallas_call x1, Pallas kernels, per_device(): pl.pallas_call(functools.partial(kernel, n_sky, n_tm), out_shape=(jax.Sha...  30.9 us
    pallas_call x1, Pallas kernels, per_device(): pl.pallas_call(hand_over, out_shape=(jax.ShapeDtypeStruct((td, rows), F32...  0.68 us

profile of v7, /device:TPU:1, one launch (start us, length us, event | category | flops | bytes accessed | tf_op | source)
XLA Modules:
  0.0 32.2 jit_solution(17269724476476384134)
XLA Ops:
  0.6 30.9 %shard_map.111 = (f32[16,128]{1,0:T(8,128)S(1)}, f32[40,128]{1,0:T(8,128)S(1)}, f32[5,4096]{1,0:T(8,128)S(1)}) custom-call(s32[16]{0:T(128)} %seg_hbm.1, s32[16]{0:T(128)} %cnt_hbm.1, f32[16,128,256]{2,1,0:T(8,128)} %tiles_hbm.1, s32[16,128]{1,0:T(8,128)} %idx_hbm.1, f32[5,16,128]{2,1,0:T(8,128)} %coef_hbm.1, f32[16,128]{1,0:T(8,128)} %wgt_hbm.1, ...), custom_call_target="tpu_custom_call" | custom-call | tf_op jit(solution)/shard_map/pallas_call | solution.py:435
  31.5 0.7 %shard_map.112 = (f32[16,128]{1,0:T(8,128)}, f32[16,256]{1,0:T(8,128)}, f32[5,4096]{1,0:T(8,128)}, f32[1]{0:T(128)}) custom-call(f32[16,128]{1,0:T(8,128)S(1)} %get-tuple-element.11.proj, f32[40,128]{1,0:T(8,128)S(1)} %get-tuple-element.12.sums, f32[5,4096]{1,0:T(8,128)S(1)} %get-tuple-element.13.src), custom_call_target="tpu_custom_call" | custom-call | tf_op jit(solution)/shard_map/pallas_call | solution.py:482
